TPU v7x, 32 devices: a whole 2x2x4 slice. The times are simulated.
32 devices in a mesh: ctx: 8 (over y, x, core), head: 4 (over z).
Axes of the slice: x: 2, y: 2, z: 4, core: 2. Of those that a mesh axis runs over, the one named last changes fastest.
Arguments:
- query_low: bfloat16 [2, 1536], P(None, 'ctx'), may hold values from -6 to 6
- query_weight: bfloat16 [1536, 73728], P('ctx', 'head'), may hold values from -0.21875 to 0.21875
- latent_cache: bfloat16 [2, 32768, 576], P(None, ('ctx', 'head')), may hold values from -300 to 300
- lengths: int32 [2], replicated, may hold values from 20481 to 32768
- value_weight: bfloat16 [128, 512, 128], P('head'), may hold values from -2 to 2
- output_weight: bfloat16 [16384, 7168], P('head', 'ctx'), may hold values from -0.0625 to 0.0625
Outputs:
- attended: bfloat16 [2, 7168], P(None, ('ctx', 'head'))
All inputs are finite; a program needn't handle non-finite values.
Results may differ from a plain program's by a relative error of at most 0.028.
Values may be sent and summed in bfloat16 or wider, within the bound.
A program may use at most 192 MiB of HBM per device.

v0:
```python
import jax
import jax.numpy as jnp
from jax import lax
from jax.sharding import PartitionSpec as P

KV_RANK = 512


softmax_scale = 0.07216878


def merged_2(x, axis, join):
    gathered = jax.tree.map(
        lambda a, kind: lax.all_gather(a.astype(kind), axis),
        x,
        (jnp.bfloat16, jnp.bfloat16, jnp.bfloat16),
    )

    def take(source):
        return jax.tree.map(
            lambda a, own: lax.dynamic_index_in_dim(a, source, 0, False).astype(own.dtype),
            gathered,
            x,
        )

    return lax.fori_loop(
        1, lax.axis_size(axis), lambda source, state: join(state, take(source)), take(0)
    )


def merge_stats(first, second):
    highest = jnp.maximum(first[0], second[0])
    first_scale = jnp.exp(first[0] - highest)
    second_scale = jnp.exp(second[0] - highest)
    totals = first[1] * first_scale + second[1] * second_scale
    numerators = first[2] * first_scale[..., None] + second[2] * second_scale[..., None]
    return (highest, totals, numerators)


def on_device(query_low, query_weight, latent_cache, lengths, value_weight, output_weight):
    head_count = lax.axis_size("head")
    sequences = query_low.shape[0]
    local_heads = value_weight.shape[0]
    all_heads = local_heads * head_count
    width = latent_cache.shape[2]
    partial_value = jnp.dot(query_low, query_weight, preferred_element_type=jnp.float32)
    summed = lax.psum(partial_value, "ctx").astype(jnp.bfloat16)
    gathered = lax.all_gather(summed, "head", axis=1, tiled=True)
    queries = gathered.reshape(sequences, all_heads, width)
    span = latent_cache.shape[1]
    offset = (lax.axis_index("ctx") * head_count + lax.axis_index("head")) * span
    places = offset + jnp.arange(span, dtype=jnp.int32)
    usable = (places[None, :] < lengths[:, None])[:, None, :]
    scores = (
        jnp.einsum("bhc,bpc->bhp", queries, latent_cache, preferred_element_type=jnp.float32)
        * softmax_scale
    )
    scores = jnp.where(usable, scores, -1e30)
    local_max = jnp.max(scores, axis=2)
    probabilities = jnp.where(usable, jnp.exp(scores - local_max[..., None]), 0.0)
    totals = jnp.sum(probabilities, axis=2)
    numerators = jnp.einsum(
        "bhp,bpc->bhc",
        probabilities.astype(jnp.bfloat16),
        latent_cache[:, :, :KV_RANK],
        preferred_element_type=jnp.float32,
    )
    merged = merged_2((local_max, totals, numerators), ("ctx", "head"), merge_stats)
    first_head = lax.axis_index("head") * local_heads
    head_totals = lax.dynamic_slice_in_dim(merged[1], first_head, local_heads, 1)
    head_numerators = lax.dynamic_slice_in_dim(merged[2], first_head, local_heads, 1)
    latent_out = (head_numerators / head_totals[..., None]).astype(jnp.bfloat16)
    values = jnp.einsum(
        "bhc,hcv->bhv", latent_out, value_weight, preferred_element_type=jnp.float32
    ).astype(jnp.bfloat16)
    projected = jnp.dot(
        values.reshape(sequences, -1), output_weight, preferred_element_type=jnp.float32
    )
    return lax.psum_scatter(projected, "head", scatter_dimension=1, tiled=True).astype(jnp.bfloat16)


def solution(mesh):
    return jax.shard_map(
        on_device,
        mesh=mesh,
        in_specs=(
            P(None, "ctx"),
            P("ctx", "head"),
            P(None, ("ctx", "head"), None),
            P(),
            P("head", None, None),
            P("head", "ctx"),
        ),
        out_specs=P(None, ("ctx", "head")),
        check_vma=False,
    )
```

profile of v0, /device:TPU:0, one launch (start us, length us, event | category | flops | bytes accessed | tf_op | source)
XLA Modules:
  0.0 260.9 jit_solution(1642688396522975280)
XLA Ops:
  7.2 4.2 %fusion.25 = f32[2,18432]{1,0:T(2,128)S(1)} fusion(bf16[2,192]{1,0:T(2,128)(2,1)S(1)} %copy-done, bf16[192,18432]{1,0:T(8,128)(2,1)} %param.9), kind=kOutput, calls=%fused_computation.40 | convolution fusion | flops 14155776 | bytes 7226112 | tf_op jit(solution)/shard_map/dot_general | solution.py:46
  11.4 27.4 %all-reduce.1 = bf16[2,18432]{1,0:T(2,128)(2,1)S(1)} all-reduce(f32[2,18432]{1,0:T(2,128)S(1)} %fusion.25), channel_id=1, replica_groups=mesh['ctx'=8,'head'=4] {'ctx'}, use_global_device_ids=true, to_apply=%region_0.0 | all-reduce | flops 36864 | bytes 221184 | tf_op jit(solution)/shard_map/psum | solution.py:47
  38.8 14.8 %all_gather.17 = bf16[2,73728]{1,0:T(2,128)(2,1)S(1)} all-gather(bf16[2,18432]{1,0:T(2,128)(2,1)S(1)} %all-reduce.1), channel_id=1, replica_groups=mesh['ctx'=8,'head'=4] {'head'}, dimensions={1}, use_global_device_ids=true | all-gather | bytes 368640 | tf_op jit(solution)/shard_map/all_gather | solution.py:48
  54.7 1.7 fusion.24
  56.4 1.6 fusion.8
  58.4 65.2 %all-gather.4 = bf16[32,2,128]{2,1,0:T(2,128)(2,1)S(1)} all-gather(bf16[1,2,128]{2,1,0:T(2,128)(2,1)S(1)} %bitcast.54), channel_id=3, replica_groups=mesh['ctx'=8,'head'=4] {'ctx','head'}, dimensions={0}, use_global_device_ids=true | all-gather | bytes 16896 | tf_op jit(solution)/shard_map/all_gather | solution.py:14
  123.6 65.0 %all-gather.3 = bf16[32,2,128]{2,1,0:T(2,128)(2,1)S(1)} all-gather(bf16[1,2,128]{2,1,0:T(2,128)(2,1)S(1)} %convert_bitcast_fusion.1), channel_id=2, replica_groups=mesh['ctx'=8,'head'=4] {'ctx','head'}, dimensions={0}, use_global_device_ids=true | all-gather | bytes 16896 | tf_op jit(solution)/shard_map/all_gather | solution.py:14
  189.6 36.4 %while.19 = (s32[]{:T(128)}, f32[2,128]{1,0:T(2,128)S(1)}, f32[2,128]{1,0:T(2,128)S(1)}, f32[2,128,512]{2,1,0:T(8,128)S(1)}, bf16[32,2,128]{2,1,0:T(2,128)(2,1)S...) while((s32[]{:T(128)}, f32[2,128]{1,0:T(2,128)S(1)}, ...), condition=%wide.region_4.5_spmd, body=%wide.region_3.4_spmd.sunk | while | flops 526341 | bytes 1320079 | solution.py:26
  189.7 1.1 fusion.35
  190.8 1.1 fusion.35
  192.0 1.1 fusion.35
  193.2 1.1 fusion.35
  196.7 1.1 fusion.35
  197.9 1.1 fusion.35
  199.1 1.1 fusion.35
  200.2 1.1 fusion.35
  204.9 1.1 fusion.35
  206.1 1.1 fusion.35
  207.3 1.1 fusion.35
  208.5 1.1 fusion.35
  212.0 1.1 fusion.35
  213.2 1.1 fusion.35
  214.3 1.1 fusion.35
  215.5 1.1 fusion.35
  219.0 1.1 fusion.35
  220.2 1.1 fusion.35
  221.4 1.1 fusion.35
  222.6 1.1 fusion.35
  224.9 1.1 fusion.35
  226.2 8.1 %convolution_bitcast_fusion = f32[896,2]{1,0:T(8,128)} fusion(bf16[4096,896]{1,0:T(8,128)(2,1)} %param.13, bf16[32,512,128]{2,1,0:T(8,128)(2,1)} %param.12, bf16[2,32,512]{2,1,0:T(8,128)(2,1)S(1)} %divide_convert_fusion), kind=kOutput, calls=%fused_computation.16 | convolution fusion | flops 23076864 | bytes 11607040
  234.4 18.1 %reduce-scatter.4.cloned.1.call-done = f32[224,2]{1,0:T(8,128)} async-done(((f32[896,2]{1,0:T(8,128)}), f32[224,2]{1,0:T(8,128)}) %reduce-scatter.4.cloned.1.call-update) | async-done | bytes 1808
  252.5 1.5 copy.18
  (62 shorter events, 15.4 us)
Async XLA Ops:
  6.5 0.7 copy-start
  6.5 182.1 %all-gather.7.cloned.1.call-start = ((), (), s32[]{:S(2)}) async-start(), calls=%async_computation.1 | async-start | bytes 8650752 | tf_op jit(solution)/shard_map/all_gather | solution.py:14
  7.2 47.4 %copy-start.2 = (s32[2]{0:T(128)S(1)}, s32[2]{0:T(128)}, u32[]{:S(2)}) copy-start(s32[2]{0:T(128)} %param.11) | copy-start | bytes 28
  7.2 47.5 %copy-start.1 = (bf16[2,1024,576]{1,2,0:T(8,128)(2,1)S(1)}, bf16[2,1024,576]{1,2,0:T(8,128)(2,1)}, u32[]{:S(2)}) copy-start(bf16[2,1024,576]{1,2,0:T(8,128)(2,1)} %param.10) | copy-start | bytes 7077892
  58.0 194.5 %reduce-scatter.4.cloned.1.call-start = ((), (), s32[]{:S(2)}) async-start(), calls=%async_computation.2 | async-start | bytes 573440
Sparse Core Ops, SparseCore 0:
  58.2 75.6 all-gather.6
  234.5 17.9 reduce-scatter.3
where the time goes:
time: 262 us; the launch traced here: 261 us
  blocking collectives  172 us (66%)
  other arithmetic  37.1 us (14%)
  waiting for transfers between devices  18.2 us (7%)
  matrix products  15.6 us (6%)
  between operations  13.4 us (5%)
  local copies, waits for them, and re-layouts  3.35 us (1%)
    all_gather x2, blocking collectives, merged_2(): lax.all_gather(a.astype(kind), axis)  130 us
    add x31, other arithmetic, merge_stats(): first[2] * first_scale[..., None] + second[2] * second_scale[..., None]  34.8 us
    psum x1, blocking collectives, on_device(): summed = lax.psum(partial_value, 'ctx').astype(jnp.bfloat16)  27.4 us
    unnamed x3, waiting for transfers between devices  18.2 us
    all_gather x1, blocking collectives, on_device(): gathered = lax.all_gather(summed, 'head', axis=1, tiled=True)  14.8 us
    unnamed x1, matrix products  8.1 us
  transfers between devices with their start and end apart: 2, of which 1 were waited for; matrix products, arithmetic and copies ran while one was open for 0% of the time, Pallas kernels for 0%

commit v1 on v0

v1 whole, which is shorter than its diff:
```python
import functools

import jax
import jax.numpy as jnp
from jax import lax
from jax.experimental import pallas as pl
from jax.experimental.pallas import tpu as pltpu
from jax.sharding import PartitionSpec as P

softmax_scale = 0.07216878
LANES = 128
F32 = jnp.float32
BF16 = jnp.bfloat16


def parts_of(x):
    high = x.astype(BF16).astype(F32)
    rest = x - high
    middle = rest.astype(BF16).astype(F32)
    return high, middle, rest - middle


def lane_sum(x, first, last):
    lane = lax.broadcasted_iota(jnp.int32, x.shape, x.ndim - 1)
    return jnp.sum(jnp.where((lane >= first) & (lane < last), x, 0.0), axis=-1, keepdims=True)


def kernel(
    ctx_count,
    head_count,
    lengths,
    query_low,
    query_weight,
    latent_cache,
    value_weight,
    output_weight,
    out,
    qw,
    cache,
    vw,
    ow,
    partial,
    partial_in,
    summed,
    query_rows,
    gathered,
    queries,
    numer,
    stat_rows,
    stat_send,
    stat_in,
    plane_send,
    plane_in,
    value_rows,
    value_all,
    projected,
    out_send,
    out_in,
    load_sem,
    qw_sem,
    p_send,
    p_recv,
    gz_send,
    gz_recv,
    gc_send,
    gc_recv,
    s_send,
    s_recv,
    z_send,
    z_recv,
    v_send,
    v_recv,
    o_send,
    o_recv,
):
    C, H = ctx_count, head_count
    me_c, me_h = lax.axis_index("ctx"), lax.axis_index("head")
    sequences = query_low.shape[0]
    pieces, depth, _ = qw.shape
    chunk = partial.shape[2]
    rows = query_rows.shape[0]
    own_heads = rows // sequences
    span, width = cache.shape[1], cache.shape[2]
    rank = vw.shape[1]
    v_dim = vw.shape[2]
    share = out.shape[1]

    def ctx_peer(step):
        return lax.rem(me_c + step, C)

    def head_peer(step):
        return lax.rem(me_h + step, H)

    def remote(source, target, send_sem, recv_sem, c, h):
        return pltpu.make_async_remote_copy(
            src_ref=source,
            dst_ref=target,
            send_sem=send_sem,
            recv_sem=recv_sem,
            device_id=(c, h),
            device_id_type=pl.DeviceIdType.MESH,
        )

    def loop(low, high, body):
        def run(i, carry):
            body(i)
            return carry

        lax.fori_loop(low, high, run, 0)

    def qw_copy(index):
        if pieces == 1:
            return pltpu.make_async_copy(query_weight, qw.at[0], qw_sem.at[0])
        columns = pl.ds(pl.multiple_of(index * chunk, LANES), chunk)
        return pltpu.make_async_copy(query_weight.at[:, columns], qw.at[index], qw_sem.at[index])

    if pieces == 1:
        qw_copy(0).start()
    else:
        loop(1, C + 1, lambda o: qw_copy(ctx_peer(o)).start())
    barrier = pltpu.get_barrier_semaphore()

    def greet(c, h):
        pl.semaphore_signal(
            barrier, inc=1, device_id=(c, h), device_id_type=pl.DeviceIdType.MESH
        )

    loop(1, C, lambda o: greet(ctx_peer(o), me_h))
    loop(1, H, lambda o: greet(me_c, head_peer(o)))
    cache_copy = pltpu.make_async_copy(latent_cache, cache, load_sem.at[0])
    cache_copy.start()
    vw_copy = pltpu.make_async_copy(
        value_weight.at[pl.ds(me_c * own_heads, own_heads)], vw, load_sem.at[1]
    )
    vw_copy.start()
    ow_copy = pltpu.make_async_copy(output_weight, ow, load_sem.at[2])
    ow_copy.start()
    pl.semaphore_wait(barrier, C + H - 2)

    def p_copy(o):
        c = ctx_peer(o)
        return remote(
            partial.at[c], partial_in.at[me_c], p_send.at[o], p_recv.at[me_c], c, me_h
        )

    def multiply(index):
        qw_copy(index).wait()
        partial[index] = jnp.dot(query_low[...], qw[index], preferred_element_type=F32)

    if pieces == 1:
        qw_copy(0).wait()
        for c in range(C):
            partial[c] = jnp.dot(
                query_low[...], qw[0, :, c * chunk : (c + 1) * chunk], preferred_element_type=F32
            )
        loop(1, C, lambda o: p_copy(o).start())
    else:

        def send_partial(o):
            multiply(ctx_peer(o))
            p_copy(o).start()

        loop(1, C, send_partial)
        multiply(me_c)
    query_rows[...] = jnp.zeros_like(query_rows)
    partial_in[me_c] = partial[me_c]

    def p_wait(o):
        c = ctx_peer(o)
        remote(partial.at[c], partial_in.at[c], p_send.at[o], p_recv.at[c], c, me_h).wait_recv()

    loop(1, C, p_wait)
    total = partial_in[0]
    for c in range(1, C):
        total = total + partial_in[c]
    summed[...] = total
    for b in range(sequences):
        for j in range(own_heads):
            row = b * own_heads + j
            query_rows[row : row + 1, 0:width] = summed[b : b + 1, j * width : (j + 1) * width]
    gathered[me_h, me_c] = query_rows[...].astype(BF16)

    def gz_copy(o):
        h = head_peer(o)
        slot = gathered.at[me_h, me_c]
        return remote(slot, slot, gz_send.at[o], gz_recv.at[me_h], me_c, h)

    def gc_copy(step, o):
        h = head_peer(step)
        slot = gathered.at[h, me_c]
        return remote(slot, slot, gc_send.at[step, o], gc_recv.at[h, me_c], ctx_peer(o), me_h)

    loop(1, H, lambda o: gz_copy(o).start())
    loop(1, C, lambda o: gc_copy(0, o).start())

    def forward(step):
        h = head_peer(step)
        slot = gathered.at[h, me_c]
        remote(slot, slot, gz_send.at[step], gz_recv.at[h], me_c, h).wait_recv()
        loop(1, C, lambda o: gc_copy(step, o).start())

    loop(1, H, forward)

    def gc_wait(step):
        def one(o):
            h, c = head_peer(step), ctx_peer(o)
            slot = gathered.at[h, c]
            remote(slot, slot, gc_send.at[step, o], gc_recv.at[h, c], c, me_h).wait_recv()

        loop(1, C, one)

    cache_copy.wait()
    loop(0, H, gc_wait)
    for h in range(H):
        for c in range(C):
            block = gathered[h, c].astype(F32)
            first = (h * C + c) * own_heads
            for b in range(sequences):
                queries[b, first : first + own_heads, :] = block[
                    b * own_heads : (b + 1) * own_heads, :
                ]

    offset = (me_c * H + me_h) * span
    all_heads = queries.shape[1]
    for b in range(sequences):
        usable = (
            offset + lax.broadcasted_iota(jnp.int32, (all_heads, span), 1)
        ) < lengths[b]
        scores = (
            lax.dot_general(
                queries[b, :, 0:width].astype(BF16),
                cache[b],
                (((1,), (1,)), ((), ())),
                preferred_element_type=F32,
            )
            * softmax_scale
        )
        scores = jnp.where(usable, scores, -1e30)
        local_max = jnp.max(scores, axis=1, keepdims=True)
        probabilities = jnp.where(usable, jnp.exp(scores - local_max), 0.0)
        totals = jnp.sum(probabilities, axis=1, keepdims=True)
        numer[b, :, 0:rank] = jnp.dot(
            probabilities.astype(BF16), cache[b, :, 0:rank], preferred_element_type=F32
        )
        lane = lax.broadcasted_iota(jnp.int32, (all_heads, LANES), 1)
        extra = jnp.zeros((all_heads, LANES), F32)
        for at, part in enumerate(parts_of(local_max) + parts_of(totals)):
            extra = jnp.where(lane == at, part, extra)
        numer[b, :, rank:] = extra
    for h in range(H):
        for c in range(C):
            first = (h * C + c) * own_heads
            for b in range(sequences):
                stat_rows[c, h, b * own_heads : (b + 1) * own_heads, :] = numer[
                    b, first : first + own_heads, :
                ]
    stat_send[...] = stat_rows[...].astype(BF16)

    def s_copy(o):
        c = ctx_peer(o)
        return remote(stat_send.at[c], stat_in.at[me_c], s_send.at[o], s_recv.at[me_c], c, me_h)

    loop(1, C, lambda o: s_copy(o).start())
    stat_in[me_c] = stat_send[me_c]

    def s_wait(o):
        c = ctx_peer(o)
        remote(stat_send.at[c], stat_in.at[c], s_send.at[o], s_recv.at[c], c, me_h).wait_recv()

    loop(1, C, s_wait)
    maxima, sums = [], []
    for c in range(C):
        extra = stat_in[c, :, :, rank:].astype(F32)
        maxima.append(lane_sum(extra, 0, 3))
        sums.append(lane_sum(extra, 3, 6))
    highest = functools.reduce(jnp.maximum, maxima)
    total, weighted = 0.0, 0.0
    for c in range(C):
        scale = jnp.exp(maxima[c] - highest)
        total = total + sums[c] * scale
        weighted = weighted + stat_in[c, :, :, 0:rank].astype(F32) * scale
    lane = lax.broadcasted_iota(jnp.int32, (H, rows, LANES), 2)
    plane_send[:, :, 0:rank] = weighted
    plane_send[:, :, rank:] = jnp.where(lane == 0, highest, jnp.where(lane == 1, total, 0.0))

    def z_copy(o):
        h = head_peer(o)
        return remote(plane_send.at[h], plane_in.at[me_h], z_send.at[o], z_recv.at[me_h], me_c, h)

    loop(1, H, lambda o: z_copy(o).start())
    plane_in[me_h] = plane_send[me_h]

    def z_wait(o):
        h = head_peer(o)
        remote(plane_send.at[h], plane_in.at[h], z_send.at[o], z_recv.at[h], me_c, h).wait_recv()

    loop(1, H, z_wait)
    maxima, sums = [], []
    for h in range(H):
        extra = plane_in[h, :, rank:]
        maxima.append(lane_sum(extra, 0, 1))
        sums.append(lane_sum(extra, 1, 2))
    highest = functools.reduce(jnp.maximum, maxima)
    total, weighted = 0.0, 0.0
    for h in range(H):
        scale = jnp.exp(maxima[h] - highest)
        total = total + sums[h] * scale
        weighted = weighted + plane_in[h, :, 0:rank] * scale
    latent_out = (weighted / total).astype(BF16)

    vw_copy.wait()
    for j in range(own_heads):
        value = jnp.dot(latent_out, vw[j], preferred_element_type=F32)
        for b in range(sequences):
            row = b * own_heads + j
            value_rows[b : b + 1, j * v_dim : (j + 1) * v_dim] = value[row : row + 1, :]
    value_all[me_c] = value_rows[...].astype(BF16)

    def v_copy(o):
        slot = value_all.at[me_c]
        return remote(slot, slot, v_send.at[o], v_recv.at[me_c], ctx_peer(o), me_h)

    loop(1, C, lambda o: v_copy(o).start())

    def v_wait(o):
        c = ctx_peer(o)
        slot = value_all.at[c]
        remote(slot, slot, v_send.at[o], v_recv.at[c], c, me_h).wait_recv()

    ow_copy.wait()
    loop(1, C, v_wait)
    block_rows = own_heads * v_dim
    projected[...] = jnp.zeros_like(projected)

    def project(c):
        at = pl.ds(pl.multiple_of(c * block_rows, block_rows), block_rows)
        projected[...] += jnp.dot(value_all[c], ow[at, :], preferred_element_type=F32)

    loop(0, C, project)
    for h in range(H):
        out_send[h] = projected[:, h * share : (h + 1) * share]

    def o_copy(o):
        h = head_peer(o)
        return remote(out_send.at[h], out_in.at[me_h], o_send.at[o], o_recv.at[me_h], me_c, h)

    loop(1, H, lambda o: o_copy(o).start())
    out_in[me_h] = out_send[me_h]

    def o_wait(o):
        h = head_peer(o)
        remote(out_send.at[h], out_in.at[h], o_send.at[o], o_recv.at[h], me_c, h).wait_recv()

    loop(1, H, o_wait)
    result = out_in[0]
    for h in range(1, H):
        result = result + out_in[h]
    out[...] = result

    loop(1, C, lambda o: p_copy(o).wait_send())
    loop(1, H, lambda o: gz_copy(o).wait_send())
    loop(0, H, lambda step: loop(1, C, lambda o: gc_copy(step, o).wait_send()))
    loop(1, C, lambda o: s_copy(o).wait_send())
    loop(1, H, lambda o: z_copy(o).wait_send())
    loop(1, C, lambda o: v_copy(o).wait_send())
    loop(1, H, lambda o: o_copy(o).wait_send())


def on_device(
    C, H, query_low, query_weight, latent_cache, lengths, value_weight, output_weight
):
    sequences = query_low.shape[0]
    local_heads, rank, v_dim = value_weight.shape
    _, span, width = latent_cache.shape
    depth, columns = query_weight.shape
    own_heads = local_heads // C
    chunk = columns // C
    rows = sequences * own_heads
    all_heads = local_heads * H
    padded = rank + LANES
    features = output_weight.shape[1]
    share = features // H
    qw_shape = (C, depth, chunk) if chunk % LANES == 0 else (1, depth, columns)
    vmem, dma = pltpu.VMEM, pltpu.SemaphoreType.DMA
    result = pl.pallas_call(
        functools.partial(kernel, C, H),
        out_shape=jax.ShapeDtypeStruct((sequences, share), F32),
        in_specs=[
            pl.BlockSpec(memory_space=pltpu.SMEM),
            pl.BlockSpec(memory_space=pltpu.VMEM),
            pl.BlockSpec(memory_space=pl.ANY),
            pl.BlockSpec(memory_space=pl.ANY),
            pl.BlockSpec(memory_space=pl.ANY),
            pl.BlockSpec(memory_space=pl.ANY),
        ],
        out_specs=pl.BlockSpec(memory_space=pltpu.VMEM),
        scratch_shapes=[
            vmem(qw_shape, BF16),
            vmem(latent_cache.shape, BF16),
            vmem((own_heads, rank, v_dim), BF16),
            vmem(output_weight.shape, BF16),
            vmem((C, sequences, chunk), F32),
            vmem((C, sequences, chunk), F32),
            vmem((sequences, chunk), F32),
            vmem((rows, padded), F32),
            vmem((H, C, rows, padded), BF16),
            vmem((sequences, all_heads, padded), F32),
            vmem((sequences, all_heads, padded), F32),
            vmem((C, H, rows, padded), F32),
            vmem((C, H, rows, padded), BF16),
            vmem((C, H, rows, padded), BF16),
            vmem((H, rows, padded), F32),
            vmem((H, rows, padded), F32),
            vmem((sequences, own_heads * v_dim), F32),
            vmem((C, sequences, own_heads * v_dim), BF16),
            vmem((sequences, features), F32),
            vmem((H, sequences, share), F32),
            vmem((H, sequences, share), F32),
            dma((3,)),
            dma((C,)),
            dma((C,)),
            dma((C,)),
            dma((H,)),
            dma((H,)),
            dma((H, C)),
            dma((H, C)),
            dma((C,)),
            dma((C,)),
            dma((H,)),
            dma((H,)),
            dma((C,)),
            dma((C,)),
            dma((H,)),
            dma((H,)),
        ],
        compiler_params=pltpu.CompilerParams(
            collective_id=0, has_side_effects=True, vmem_limit_bytes=48 * 1024 * 1024
        ),
    )(lengths, query_low, query_weight, latent_cache, value_weight, output_weight)
    return result.astype(BF16)


def solution(mesh):
    return jax.shard_map(
        functools.partial(on_device, mesh.shape["ctx"], mesh.shape["head"]),
        mesh=mesh,
        in_specs=(
            P(None, "ctx"),
            P("ctx", "head"),
            P(None, ("ctx", "head"), None),
            P(),
            P("head", None, None),
            P("head", "ctx"),
        ),
        out_specs=P(None, ("ctx", "head")),
        check_vma=False,
    )
```

time: 262 us -> 44.2 us (0.17)
  blocking collectives: 172 us -> 0 us
  Pallas kernels: 0 us -> 40.3 us
  other arithmetic: 37.1 us -> 0.56 us
  waiting for transfers between devices: 18.2 us -> 0 us
  matrix products: 15.6 us -> 0 us
  between operations: 13.4 us -> 0.03 us
    all_gather x3 -> x0, blocking collectives: 145 us -> none  [the longest x2 130 us: merged_2(): lax.all_gather(a.astype(kind), axis)]
    pallas_call x0 -> x1, Pallas kernels: none -> 40.3 us  [on_device(): pl.pallas_call(functools.partial(kernel, C, H), out_shape=jax.ShapeDtypeS...]
    add x63 -> x0, other arithmetic: 35.6 us -> none  [the longest x31 34.8 us: merge_stats(): first[2] * first_scale[..., None] + second[2] * second_scale[..., None]]
    psum x1 -> x0, blocking collectives: 27.4 us -> none  [on_device(): summed = lax.psum(partial_value, 'ctx').astype(jnp.bfloat16)]
    unnamed x3 -> x0, waiting for transfers between devices: 18.2 us -> none
    unnamed x1 -> x0, matrix products: 8.1 us -> none
    dot_general x3 -> x0, matrix products: 7.47 us -> none  [the longest x1 4.18 us: on_device(): jnp.dot(query_low, query_weight, preferred_element_type=jnp.float32)]
  transfers between devices with their start and end apart: 2 -> 0, of which waited for: 1 -> 0; matrix products, arithmetic and copies ran while one was open for 0% -> 0% of each run, Pallas kernels for 0% -> 0%
where the time goes in v1:
time: 44.2 us; the launch traced here: 44 us
  Pallas kernels  40.3 us (91%)
  local copies, waits for them, and re-layouts  3.12 us (7%)
  other arithmetic  0.56 us (1%)
    pallas_call x1, Pallas kernels, on_device(): pl.pallas_call(functools.partial(kernel, C, H), out_shape=jax.ShapeDtypeS...  40.3 us
    unnamed x5, local copies, waits for them, and re-layouts  3.12 us

profile of v1, /device:TPU:0, one launch (start us, length us, event | category | flops | bytes accessed | tf_op | source)
XLA Modules:
  0.0 44.0 jit_solution(4107148851350897857)
XLA Ops:
  0.0 0.0 copy-start.1
  0.0 0.0 copy-start
  0.0 3.1 %copy.7.latent_cache = bf16[2,1024,576]{2,1,0:T(8,128)(2,1)S(1)} copy(bf16[2,1024,576]{1,2,0:T(8,128)(2,1)} %param.8) | data formatting | bytes 4718592 | tf_op args[2]
  3.1 0.0 copy-done.1
  3.1 0.0 copy-done
  3.1 40.3 %shard_map.64 = f32[2,224]{1,0:T(2,128)S(1)} custom-call(s32[2]{0:T(128)S(1)} %copy-done.1, bf16[2,192]{1,0:T(2,128)(2,1)S(1)} %copy-done, bf16[192,18432]{1,0:T(8,128)(2,1)} %query_weight.1, bf16[2,1024,576]{2,1,0:T(8,128)(2,1)S(1)} %copy.7.latent_cache, bf16[32,512,128]{2,1,0:T(8,128)(2,1)} %value_weight.1, bf16[4096,896]{1,0:T(8,128)(2,1)} %output_weight.1), custom_call_target="tpu_custom_call" | custom-call | tf_op jit(solution)/shard_map/pallas_call | solution.py:385
  43.5 0.6 %convert_element_type.3 = bf16[2,224]{1,0:T(2,128)(2,1)} convert(f32[2,224]{1,0:T(2,128)S(1)} %shard_map.64) | non-fusion elementwise | flops 448 | bytes 2688 | tf_op jit(solution)/shard_map/convert_element_type | solution.py:440
Async XLA Ops:
  0.0 3.1 %copy-start.1 = (s32[2]{0:T(128)S(1)}, s32[2]{0:T(128)}, u32[]{:S(2)}) copy-start(s32[2]{0:T(128)} %lengths.1) | copy-start | bytes 28
  0.0 3.1 %copy-start = (bf16[2,192]{1,0:T(2,128)(2,1)S(1)}, bf16[2,192]{1,0:T(2,128)(2,1)}, u32[]{:S(2)}) copy-start(bf16[2,192]{1,0:T(2,128)(2,1)} %query_low.1) | copy-start | bytes 2308

commit v2 on v1

--- a/solution.py
+++ b/solution.py
@@ -46,7 +46,7 @@
     gathered,
     queries,
     numer,
-    stat_rows,
+    latent_rows,
     stat_send,
     stat_in,
     plane_send,
@@ -78,9 +78,8 @@
     sequences = query_low.shape[0]
     pieces, depth, _ = qw.shape
     chunk = partial.shape[2]
-    rows = query_rows.shape[0]
-    own_heads = rows // sequences
-    span, width = cache.shape[1], cache.shape[2]
+    own_heads = query_rows.shape[1]
+    width, span = cache.shape[1], cache.shape[2]
     rank = vw.shape[1]
     v_dim = vw.shape[2]
     share = out.shape[1]
@@ -128,14 +127,10 @@
     loop(1, C, lambda o: greet(ctx_peer(o), me_h))
     loop(1, H, lambda o: greet(me_c, head_peer(o)))
     cache_copy = pltpu.make_async_copy(latent_cache, cache, load_sem.at[0])
-    cache_copy.start()
     vw_copy = pltpu.make_async_copy(
         value_weight.at[pl.ds(me_c * own_heads, own_heads)], vw, load_sem.at[1]
     )
-    vw_copy.start()
     ow_copy = pltpu.make_async_copy(output_weight, ow, load_sem.at[2])
-    ow_copy.start()
-    pl.semaphore_wait(barrier, C + H - 2)
 
     def p_copy(o):
         c = ctx_peer(o)
@@ -153,15 +148,20 @@
             partial[c] = jnp.dot(
                 query_low[...], qw[0, :, c * chunk : (c + 1) * chunk], preferred_element_type=F32
             )
+        pl.semaphore_wait(barrier, C + H - 2)
         loop(1, C, lambda o: p_copy(o).start())
     else:
 
         def send_partial(o):
-            multiply(ctx_peer(o))
             p_copy(o).start()
-
+            multiply(ctx_peer(o + 1))
+
+        multiply(ctx_peer(1))
+        pl.semaphore_wait(barrier, C + H - 2)
         loop(1, C, send_partial)
-        multiply(me_c)
+    cache_copy.start()
+    vw_copy.start()
+    ow_copy.start()
     query_rows[...] = jnp.zeros_like(query_rows)
     partial_in[me_c] = partial[me_c]
 
@@ -176,62 +176,62 @@
     summed[...] = total
     for b in range(sequences):
         for j in range(own_heads):
-            row = b * own_heads + j
-            query_rows[row : row + 1, 0:width] = summed[b : b + 1, j * width : (j + 1) * width]
-    gathered[me_h, me_c] = query_rows[...].astype(BF16)
-
-    def gz_copy(o):
+            query_rows[b, j : j + 1, 0:width] = summed[b : b + 1, j * width : (j + 1) * width]
+        gathered[b, me_h, me_c] = query_rows[b].astype(BF16)
+
+    def gz_copy(b, o):
         h = head_peer(o)
-        slot = gathered.at[me_h, me_c]
-        return remote(slot, slot, gz_send.at[o], gz_recv.at[me_h], me_c, h)
-
-    def gc_copy(step, o):
+        slot = gathered.at[b, me_h, me_c]
+        return remote(slot, slot, gz_send.at[b, o], gz_recv.at[b, me_h], me_c, h)
+
+    def gc_copy(b, step, o):
         h = head_peer(step)
-        slot = gathered.at[h, me_c]
-        return remote(slot, slot, gc_send.at[step, o], gc_recv.at[h, me_c], ctx_peer(o), me_h)
-
-    loop(1, H, lambda o: gz_copy(o).start())
-    loop(1, C, lambda o: gc_copy(0, o).start())
-
-    def forward(step):
+        slot = gathered.at[b, h, me_c]
+        return remote(
+            slot, slot, gc_send.at[b, step, o], gc_recv.at[b, h, me_c], ctx_peer(o), me_h
+        )
+
+    def forward(b, step):
         h = head_peer(step)
-        slot = gathered.at[h, me_c]
-        remote(slot, slot, gz_send.at[step], gz_recv.at[h], me_c, h).wait_recv()
-        loop(1, C, lambda o: gc_copy(step, o).start())
-
-    loop(1, H, forward)
-
-    def gc_wait(step):
+        slot = gathered.at[b, h, me_c]
+        remote(slot, slot, gz_send.at[b, step], gz_recv.at[b, h], me_c, h).wait_recv()
+        loop(1, C, lambda o: gc_copy(b, step, o).start())
+
+    def gc_wait(b, step):
         def one(o):
             h, c = head_peer(step), ctx_peer(o)
-            slot = gathered.at[h, c]
-            remote(slot, slot, gc_send.at[step, o], gc_recv.at[h, c], c, me_h).wait_recv()
+            slot = gathered.at[b, h, c]
+            remote(slot, slot, gc_send.at[b, step, o], gc_recv.at[b, h, c], c, me_h).wait_recv()
 
         loop(1, C, one)
 
+    for b in range(sequences):
+        loop(1, H, lambda o: gz_copy(b, o).start())
+        loop(1, C, lambda o: gc_copy(b, 0, o).start())
+    for b in range(sequences):
+        loop(1, H, lambda step: forward(b, step))
     cache_copy.wait()
-    loop(0, H, gc_wait)
-    for h in range(H):
-        for c in range(C):
-            block = gathered[h, c].astype(F32)
-            first = (h * C + c) * own_heads
-            for b in range(sequences):
-                queries[b, first : first + own_heads, :] = block[
-                    b * own_heads : (b + 1) * own_heads, :
-                ]
+
+    def s_copy(b, o):
+        c = ctx_peer(o)
+        return remote(
+            stat_send.at[b, c], stat_in.at[b, me_c], s_send.at[b, o], s_recv.at[b, me_c], c, me_h
+        )
 
     offset = (me_c * H + me_h) * span
     all_heads = queries.shape[1]
     for b in range(sequences):
+        loop(0, H, lambda step: gc_wait(b, step))
+        for h in range(H):
+            for c in range(C):
+                first = (h * C + c) * own_heads
+                queries[b, first : first + own_heads, :] = gathered[b, h, c].astype(F32)
         usable = (
             offset + lax.broadcasted_iota(jnp.int32, (all_heads, span), 1)
         ) < lengths[b]
         scores = (
-            lax.dot_general(
-                queries[b, :, 0:width].astype(BF16),
-                cache[b],
-                (((1,), (1,)), ((), ())),
-                preferred_element_type=F32,
+            jnp.dot(
+                queries[b, :, 0:width].astype(BF16), cache[b], preferred_element_type=F32
             )
             * softmax_scale
         )
@@ -239,74 +239,77 @@
         local_max = jnp.max(scores, axis=1, keepdims=True)
         probabilities = jnp.where(usable, jnp.exp(scores - local_max), 0.0)
         totals = jnp.sum(probabilities, axis=1, keepdims=True)
-        numer[b, :, 0:rank] = jnp.dot(
-            probabilities.astype(BF16), cache[b, :, 0:rank], preferred_element_type=F32
+        numer[b, :, 0:rank] = lax.dot_general(
+            probabilities.astype(BF16),
+            cache[b, 0:rank, :],
+            (((1,), (1,)), ((), ())),
+            preferred_element_type=F32,
         )
         lane = lax.broadcasted_iota(jnp.int32, (all_heads, LANES), 1)
         extra = jnp.zeros((all_heads, LANES), F32)
         for at, part in enumerate(parts_of(local_max) + parts_of(totals)):
             extra = jnp.where(lane == at, part, extra)
         numer[b, :, rank:] = extra
-    for h in range(H):
+        for h in range(H):
+            for c in range(C):
+                first = (h * C + c) * own_heads
+                stat_send[b, c, h] = numer[b, first : first + own_heads, :].astype(BF16)
+        loop(1, C, lambda o: s_copy(b, o).start())
+        stat_in[b, me_c] = stat_send[b, me_c]
+
+    def s_wait(b, o):
+        c = ctx_peer(o)
+        remote(
+            stat_send.at[b, c], stat_in.at[b, c], s_send.at[b, o], s_recv.at[b, c], c, me_h
+        ).wait_recv()
+
+    def z_copy(b, o):
+        h = head_peer(o)
+        return remote(
+            plane_send.at[b, h], plane_in.at[b, me_h], z_send.at[b, o], z_recv.at[b, me_h], me_c, h
+        )
+
+    def z_wait(b, o):
+        h = head_peer(o)
+        remote(
+            plane_send.at[b, h], plane_in.at[b, h], z_send.at[b, o], z_recv.at[b, h], me_c, h
+        ).wait_recv()
+
+    for b in range(sequences):
+        loop(1, C, lambda o: s_wait(b, o))
+        maxima, sums = [], []
         for c in range(C):
-            first = (h * C + c) * own_heads
-            for b in range(sequences):
-                stat_rows[c, h, b * own_heads : (b + 1) * own_heads, :] = numer[
-                    b, first : first + own_heads, :
-                ]
-    stat_send[...] = stat_rows[...].astype(BF16)
-
-    def s_copy(o):
-        c = ctx_peer(o)
-        return remote(stat_send.at[c], stat_in.at[me_c], s_send.at[o], s_recv.at[me_c], c, me_h)
-
-    loop(1, C, lambda o: s_copy(o).start())
-    stat_in[me_c] = stat_send[me_c]
-
-    def s_wait(o):
-        c = ctx_peer(o)
-        remote(stat_send.at[c], stat_in.at[c], s_send.at[o], s_recv.at[c], c, me_h).wait_recv()
-
-    loop(1, C, s_wait)
-    maxima, sums = [], []
-    for c in range(C):
-        extra = stat_in[c, :, :, rank:].astype(F32)
-        maxima.append(lane_sum(extra, 0, 3))
-        sums.append(lane_sum(extra, 3, 6))
-    highest = functools.reduce(jnp.maximum, maxima)
-    total, weighted = 0.0, 0.0
-    for c in range(C):
-        scale = jnp.exp(maxima[c] - highest)
-        total = total + sums[c] * scale
-        weighted = weighted + stat_in[c, :, :, 0:rank].astype(F32) * scale
-    lane = lax.broadcasted_iota(jnp.int32, (H, rows, LANES), 2)
-    plane_send[:, :, 0:rank] = weighted
-    plane_send[:, :, rank:] = jnp.where(lane == 0, highest, jnp.where(lane == 1, total, 0.0))
-
-    def z_copy(o):
-        h = head_peer(o)
-        return remote(plane_send.at[h], plane_in.at[me_h], z_send.at[o], z_recv.at[me_h], me_c, h)
-
-    loop(1, H, lambda o: z_copy(o).start())
-    plane_in[me_h] = plane_send[me_h]
-
-    def z_wait(o):
-        h = head_peer(o)
-        remote(plane_send.at[h], plane_in.at[h], z_send.at[o], z_recv.at[h], me_c, h).wait_recv()
-
-    loop(1, H, z_wait)
-    maxima, sums = [], []
-    for h in range(H):
-        extra = plane_in[h, :, rank:]
-        maxima.append(lane_sum(extra, 0, 1))
-        sums.append(lane_sum(extra, 1, 2))
-    highest = functools.reduce(jnp.maximum, maxima)
-    total, weighted = 0.0, 0.0
-    for h in range(H):
-        scale = jnp.exp(maxima[h] - highest)
-        total = total + sums[h] * scale
-        weighted = weighted + plane_in[h, :, 0:rank] * scale
-    latent_out = (weighted / total).astype(BF16)
+            extra = stat_in[b, c, :, :, rank:].astype(F32)
+            maxima.append(lane_sum(extra, 0, 3))
+            sums.append(lane_sum(extra, 3, 6))
+        highest = functools.reduce(jnp.maximum, maxima)
+        total, weighted = 0.0, 0.0
+        for c in range(C):
+            scale = jnp.exp(maxima[c] - highest)
+            total = total + sums[c] * scale
+            weighted = weighted + stat_in[b, c, :, :, 0:rank].astype(F32) * scale
+        lane = lax.broadcasted_iota(jnp.int32, (H, own_heads, LANES), 2)
+        plane_send[b, :, :, 0:rank] = weighted
+        plane_send[b, :, :, rank:] = jnp.where(
+            lane == 0, highest, jnp.where(lane == 1, total, 0.0)
+        )
+        loop(1, H, lambda o: z_copy(b, o).start())
+        plane_in[b, me_h] = plane_send[b, me_h]
+    for b in range(sequences):
+        loop(1, H, lambda o: z_wait(b, o))
+        maxima, sums = [], []
+        for h in range(H):
+            extra = plane_in[b, h, :, rank:]
+            maxima.append(lane_sum(extra, 0, 1))
+            sums.append(lane_sum(extra, 1, 2))
+        highest = functools.reduce(jnp.maximum, maxima)
+        total, weighted = 0.0, 0.0
+        for h in range(H):
+            scale = jnp.exp(maxima[h] - highest)
+            total = total + sums[h] * scale
+            weighted = weighted + plane_in[b, h, :, 0:rank] * scale
+        latent_rows[b * own_heads : (b + 1) * own_heads, :] = weighted / total
+    latent_out = latent_rows[...].astype(BF16)
 
     vw_copy.wait()
     for j in range(own_heads):
@@ -328,7 +331,6 @@
         remote(slot, slot, v_send.at[o], v_recv.at[c], c, me_h).wait_recv()
 
     ow_copy.wait()
-    loop(1, C, v_wait)
     block_rows = own_heads * v_dim
     projected[...] = jnp.zeros_like(projected)
 
@@ -336,7 +338,12 @@
         at = pl.ds(pl.multiple_of(c * block_rows, block_rows), block_rows)
         projected[...] += jnp.dot(value_all[c], ow[at, :], preferred_element_type=F32)
 
-    loop(0, C, project)
+    def project_next(o):
+        v_wait(o)
+        project(ctx_peer(o))
+
+    project(me_c)
+    loop(1, C, project_next)
     for h in range(H):
         out_send[h] = projected[:, h * share : (h + 1) * share]
 
@@ -358,10 +365,11 @@
     out[...] = result
 
     loop(1, C, lambda o: p_copy(o).wait_send())
-    loop(1, H, lambda o: gz_copy(o).wait_send())
-    loop(0, H, lambda step: loop(1, C, lambda o: gc_copy(step, o).wait_send()))
-    loop(1, C, lambda o: s_copy(o).wait_send())
-    loop(1, H, lambda o: z_copy(o).wait_send())
+    for b in range(sequences):
+        loop(1, H, lambda o: gz_copy(b, o).wait_send())
+        loop(0, H, lambda step: loop(1, C, lambda o: gc_copy(b, step, o).wait_send()))
+        loop(1, C, lambda o: s_copy(b, o).wait_send())
+        loop(1, H, lambda o: z_copy(b, o).wait_send())
     loop(1, C, lambda o: v_copy(o).wait_send())
     loop(1, H, lambda o: o_copy(o).wait_send())
 
@@ -369,13 +377,12 @@
 def on_device(
     C, H, query_low, query_weight, latent_cache, lengths, value_weight, output_weight
 ):
+    latent_cache = jnp.swapaxes(latent_cache, 1, 2)
     sequences = query_low.shape[0]
     local_heads, rank, v_dim = value_weight.shape
-    _, span, width = latent_cache.shape
     depth, columns = query_weight.shape
     own_heads = local_heads // C
     chunk = columns // C
-    rows = sequences * own_heads
     all_heads = local_heads * H
     padded = rank + LANES
     features = output_weight.shape[1]
@@ -402,15 +409,15 @@
             vmem((C, sequences, chunk), F32),
             vmem((C, sequences, chunk), F32),
             vmem((sequences, chunk), F32),
-            vmem((rows, padded), F32),
-            vmem((H, C, rows, padded), BF16),
+            vmem((sequences, own_heads, padded), F32),
+            vmem((sequences, H, C, own_heads, padded), BF16),
             vmem((sequences, all_heads, padded), F32),
             vmem((sequences, all_heads, padded), F32),
-            vmem((C, H, rows, padded), F32),
-            vmem((C, H, rows, padded), BF16),
-            vmem((C, H, rows, padded), BF16),
-            vmem((H, rows, padded), F32),
-            vmem((H, rows, padded), F32),
+            vmem((sequences * own_heads, rank), F32),
+            vmem((sequences, C, H, own_heads, padded), BF16),
+            vmem((sequences, C, H, own_heads, padded), BF16),
+            vmem((sequences, H, own_heads, padded), F32),
+            vmem((sequences, H, own_heads, padded), F32),
             vmem((sequences, own_heads * v_dim), F32),
             vmem((C, sequences, own_heads * v_dim), BF16),
             vmem((sequences, features), F32),
@@ -420,14 +427,14 @@
             dma((C,)),
             dma((C,)),
             dma((C,)),
-            dma((H,)),
-            dma((H,)),
-            dma((H, C)),
-            dma((H, C)),
-            dma((C,)),
-            dma((C,)),
-            dma((H,)),
-            dma((H,)),
+            dma((sequences, H)),
+            dma((sequences, H)),
+            dma((sequences, H, C)),
+            dma((sequences, H, C)),
+            dma((sequences, C)),
+            dma((sequences, C)),
+            dma((sequences, H)),
+            dma((sequences, H)),
             dma((C,)),
             dma((C,)),
             dma((H,)),

time: 44.2 us -> 42.3 us (0.957)
  Pallas kernels: 40.3 us -> 38.5 us
    pallas_call x1, Pallas kernels: 40.3 us -> 38.5 us  [on_device(): pl.pallas_call(functools.partial(kernel, C, H), out_shape=jax.ShapeDtypeS...]
    unnamed x5 -> x6, local copies, waits for them, and re-layouts: 3.12 us -> 3 us
where the time goes in v2:
time: 42.3 us; the launch traced here: 42.1 us
  Pallas kernels  38.5 us (91%)
  local copies, waits for them, and re-layouts  3 us (7%)
  other arithmetic  0.56 us (1%)
    pallas_call x1, Pallas kernels, on_device(): pl.pallas_call(functools.partial(kernel, C, H), out_shape=jax.ShapeDtypeS...  38.5 us
    unnamed x6, local copies, waits for them, and re-layouts  3 us

profile of v2, /device:TPU:0, one launch (start us, length us, event | category | flops | bytes accessed | tf_op | source)
XLA Modules:
  0.0 42.1 jit_solution(1213201600438863875)
XLA Ops:
  0.0 0.0 copy-start
  0.0 1.7 %copy-done = bf16[2,1024,576]{1,2,0:T(8,128)(2,1)S(1)} copy-done((bf16[2,1024,576]{1,2,0:T(8,128)(2,1)S(1)}, bf16[2,1024,576]{1,2,0:T(8,128)(2,1)}, u32[]{:S(2)}) %copy-start) | copy-done | bytes 2359320
  1.7 0.0 copy-start.1
  1.7 0.7 %copy-done.1 = bf16[2,192]{1,0:T(2,128)(2,1)S(1)} copy-done((bf16[2,192]{1,0:T(2,128)(2,1)S(1)}, bf16[2,192]{1,0:T(2,128)(2,1)}, u32[]{:S(2)}) %copy-start.1) | copy-done | bytes 792
  2.3 0.0 copy-start.2
  2.3 0.7 %copy-done.2 = s32[2]{0:T(128)S(1)} copy-done((s32[2]{0:T(128)S(1)}, s32[2]{0:T(128)}, u32[]{:S(2)}) %copy-start.2) | copy-done | bytes 32
  3.0 38.5 %shard_map.64 = f32[2,224]{1,0:T(2,128)S(1)} custom-call(s32[2]{0:T(128)S(1)} %copy-done.2, bf16[2,192]{1,0:T(2,128)(2,1)S(1)} %copy-done.1, bf16[192,18432]{1,0:T(8,128)(2,1)} %query_weight.1, bf16[2,576,1024]{2,1,0:T(8,128)(2,1)S(1)} %bitcast.1, bf16[32,512,128]{2,1,0:T(8,128)(2,1)} %value_weight.1, bf16[4096,896]{1,0:T(8,128)(2,1)} %output_weight.1), custom_call_target="tpu_custom_call" | custom-call | tf_op jit(solution)/shard_map/pallas_call | solution.py:392
  41.6 0.6 %convert_element_type.3 = bf16[2,224]{1,0:T(2,128)(2,1)} convert(f32[2,224]{1,0:T(2,128)S(1)} %shard_map.64) | non-fusion elementwise | flops 448 | bytes 2688 | tf_op jit(solution)/shard_map/convert_element_type | solution.py:447
Async XLA Ops:
  0.0 1.7 %copy-start = (bf16[2,1024,576]{1,2,0:T(8,128)(2,1)S(1)}, bf16[2,1024,576]{1,2,0:T(8,128)(2,1)}, u32[]{:S(2)}) copy-start(bf16[2,1024,576]{1,2,0:T(8,128)(2,1)} %param.8) | copy-start | bytes 7077892
  1.7 0.7 %copy-start.1 = (bf16[2,192]{1,0:T(2,128)(2,1)S(1)}, bf16[2,192]{1,0:T(2,128)(2,1)}, u32[]{:S(2)}) copy-start(bf16[2,192]{1,0:T(2,128)(2,1)} %query_low.1) | copy-start | bytes 2308
  2.3 0.7 %copy-start.2 = (s32[2]{0:T(128)S(1)}, s32[2]{0:T(128)}, u32[]{:S(2)}) copy-start(s32[2]{0:T(128)} %lengths.1) | copy-start | bytes 28

commit v3 on v2

--- a/solution.py
+++ b/solution.py
@@ -28,13 +28,16 @@
 def kernel(
     ctx_count,
     head_count,
-    lengths,
-    query_low,
+    lengths_from,
+    query_low_from,
     query_weight,
     latent_cache,
     value_weight,
     output_weight,
     out,
+    lengths,
+    query_low,
+    spread,
     qw,
     cache,
     vw,
@@ -113,25 +116,40 @@
         columns = pl.ds(pl.multiple_of(index * chunk, LANES), chunk)
         return pltpu.make_async_copy(query_weight.at[:, columns], qw.at[index], qw_sem.at[index])
 
+    barrier = pltpu.get_barrier_semaphore()
+
+    def greet(c, h):
+        pl.semaphore_signal(
+            barrier, inc=1, device_id=(c, h), device_id_type=pl.DeviceIdType.MESH
+        )
+
+    loop(1, H, lambda o: greet(me_c, head_peer(o)))
+    loop(1, C, lambda o: greet(ctx_peer(o), me_h))
+
+    lengths_copy = pltpu.make_async_copy(lengths_from, lengths, load_sem.at[3])
+    low_copy = pltpu.make_async_copy(query_low_from, query_low, load_sem.at[4])
+    low_copy.start()
+    lengths_copy.start()
     if pieces == 1:
         qw_copy(0).start()
     else:
         loop(1, C + 1, lambda o: qw_copy(ctx_peer(o)).start())
-    barrier = pltpu.get_barrier_semaphore()
-
-    def greet(c, h):
-        pl.semaphore_signal(
-            barrier, inc=1, device_id=(c, h), device_id_type=pl.DeviceIdType.MESH
-        )
-
-    loop(1, C, lambda o: greet(ctx_peer(o), me_h))
-    loop(1, H, lambda o: greet(me_c, head_peer(o)))
     cache_copy = pltpu.make_async_copy(latent_cache, cache, load_sem.at[0])
     vw_copy = pltpu.make_async_copy(
         value_weight.at[pl.ds(me_c * own_heads, own_heads)], vw, load_sem.at[1]
     )
     ow_copy = pltpu.make_async_copy(output_weight, ow, load_sem.at[2])
 
+    low_copy.wait()
+    for b in range(sequences):
+        pick = lax.broadcasted_iota(jnp.int32, (sequences, LANES), 0) == b
+        spread[b] = lax.dot_general(
+            query_low[...],
+            jnp.where(pick, 1.0, 0.0).astype(BF16),
+            (((0,), (0,)), ((), ())),
+            preferred_element_type=F32,
+        )
+
     def p_copy(o):
         c = ctx_peer(o)
         return remote(
@@ -140,7 +158,12 @@
 
     def multiply(index):
         qw_copy(index).wait()
-        partial[index] = jnp.dot(query_low[...], qw[index], preferred_element_type=F32)
+        for at in range(0, chunk, LANES):
+            weight = qw[index, :, at : at + LANES].astype(F32)
+            for b in range(sequences):
+                partial[index, b : b + 1, at : at + LANES] = jnp.sum(
+                    weight * spread[b], axis=0, keepdims=True
+                )
 
     if pieces == 1:
         qw_copy(0).wait()
@@ -218,6 +241,7 @@
             stat_send.at[b, c], stat_in.at[b, me_c], s_send.at[b, o], s_recv.at[b, me_c], c, me_h
         )
 
+    lengths_copy.wait()
     offset = (me_c * H + me_h) * span
     all_heads = queries.shape[1]
     for b in range(sequences):
@@ -393,15 +417,18 @@
         functools.partial(kernel, C, H),
         out_shape=jax.ShapeDtypeStruct((sequences, share), F32),
         in_specs=[
-            pl.BlockSpec(memory_space=pltpu.SMEM),
-            pl.BlockSpec(memory_space=pltpu.VMEM),
-            pl.BlockSpec(memory_space=pl.ANY),
-            pl.BlockSpec(memory_space=pl.ANY),
-            pl.BlockSpec(memory_space=pl.ANY),
-            pl.BlockSpec(memory_space=pl.ANY),
+            pl.BlockSpec(memory_space=pltpu.HBM),
+            pl.BlockSpec(memory_space=pltpu.HBM),
+            pl.BlockSpec(memory_space=pltpu.HBM),
+            pl.BlockSpec(memory_space=pltpu.HBM),
+            pl.BlockSpec(memory_space=pltpu.HBM),
+            pl.BlockSpec(memory_space=pltpu.HBM),
         ],
         out_specs=pl.BlockSpec(memory_space=pltpu.VMEM),
         scratch_shapes=[
+            pltpu.SMEM((sequences,), jnp.int32),
+            vmem(query_low.shape, BF16),
+            vmem((sequences, depth, LANES), F32),
             vmem(qw_shape, BF16),
             vmem(latent_cache.shape, BF16),
             vmem((own_heads, rank, v_dim), BF16),
@@ -423,7 +450,7 @@
             vmem((sequences, features), F32),
             vmem((H, sequences, share), F32),
             vmem((H, sequences, share), F32),
-            dma((3,)),
+            dma((5,)),
             dma((C,)),
             dma((C,)),
             dma((C,)),
@@ -441,7 +468,7 @@
             dma((H,)),
         ],
         compiler_params=pltpu.CompilerParams(
-            collective_id=0, has_side_effects=True, vmem_limit_bytes=48 * 1024 * 1024
+            collective_id=0, has_side_effects=True, vmem_limit_bytes=60 * 1024 * 1024
         ),
     )(lengths, query_low, query_weight, latent_cache, value_weight, output_weight)
     return result.astype(BF16)

time: 42.3 us -> 40.4 us (0.955)
  local copies, waits for them, and re-layouts: 3 us -> 0 us
  other arithmetic: 0.56 us -> 1.25 us
  Pallas kernels: 38.5 us -> 39 us
    unnamed x6 -> x0, local copies, waits for them, and re-layouts: 3 us -> none
    convert_element_type x1, other arithmetic: 0.56 us -> 1.25 us  [on_device(): return result.astype(BF16)]
where the time goes in v3:
time: 40.4 us; the launch traced here: 40.2 us
  Pallas kernels  39 us (97%)
  other arithmetic  1.25 us (3%)
    pallas_call x1, Pallas kernels, on_device(): pl.pallas_call(functools.partial(kernel, C, H), out_shape=jax.ShapeDtypeS...  39 us
    convert_element_type x1, other arithmetic, on_device(): return result.astype(BF16)  1.25 us

profile of v3, /device:TPU:0, one launch (start us, length us, event | category | flops | bytes accessed | tf_op | source)
XLA Modules:
  0.0 40.2 jit_solution(3019108709337673291)
XLA Ops:
  0.0 39.0 %shard_map.64 = f32[2,224]{1,0:T(2,128)} custom-call(s32[2]{0:T(128)} %lengths_from.1, bf16[2,192]{1,0:T(2,128)(2,1)} %query_low_from.1, bf16[192,18432]{1,0:T(8,128)(2,1)} %query_weight.1, bf16[2,576,1024]{2,1,0:T(8,128)(2,1)} %bitcast.1, bf16[32,512,128]{2,1,0:T(8,128)(2,1)} %value_weight.1, bf16[4096,896]{1,0:T(8,128)(2,1)} %output_weight.1), custom_call_target="tpu_custom_call" | custom-call | tf_op jit(solution)/shard_map/pallas_call | solution.py:416
  39.0 1.2 %convert_element_type.3 = bf16[2,224]{1,0:T(2,128)(2,1)} convert(f32[2,224]{1,0:T(2,128)} %shard_map.64) | non-fusion elementwise | flops 448 | bytes 2688 | tf_op jit(solution)/shard_map/convert_element_type | solution.py:474

commit v4 on v3

--- a/solution.py
+++ b/solution.py
@@ -200,39 +200,37 @@
     for b in range(sequences):
         for j in range(own_heads):
             query_rows[b, j : j + 1, 0:width] = summed[b : b + 1, j * width : (j + 1) * width]
-        gathered[b, me_h, me_c] = query_rows[b].astype(BF16)
-
-    def gz_copy(b, o):
+        gathered[me_h, me_c, b] = query_rows[b].astype(BF16)
+
+    def gz_copy(o):
         h = head_peer(o)
-        slot = gathered.at[b, me_h, me_c]
-        return remote(slot, slot, gz_send.at[b, o], gz_recv.at[b, me_h], me_c, h)
-
-    def gc_copy(b, step, o):
+        slot = gathered.at[me_h, me_c]
+        return remote(slot, slot, gz_send.at[o], gz_recv.at[me_h], me_c, h)
+
+    def gc_copy(step, o):
         h = head_peer(step)
-        slot = gathered.at[b, h, me_c]
+        slot = gathered.at[h, me_c]
         return remote(
-            slot, slot, gc_send.at[b, step, o], gc_recv.at[b, h, me_c], ctx_peer(o), me_h
-        )
-
-    def forward(b, step):
+            slot, slot, gc_send.at[step, o], gc_recv.at[h, me_c], ctx_peer(o), me_h
+        )
+
+    def forward(step):
         h = head_peer(step)
-        slot = gathered.at[b, h, me_c]
-        remote(slot, slot, gz_send.at[b, step], gz_recv.at[b, h], me_c, h).wait_recv()
-        loop(1, C, lambda o: gc_copy(b, step, o).start())
-
-    def gc_wait(b, step):
+        slot = gathered.at[h, me_c]
+        remote(slot, slot, gz_send.at[step], gz_recv.at[h], me_c, h).wait_recv()
+        loop(1, C, lambda o: gc_copy(step, o).start())
+
+    def gc_wait(step):
         def one(o):
             h, c = head_peer(step), ctx_peer(o)
-            slot = gathered.at[b, h, c]
-            remote(slot, slot, gc_send.at[b, step, o], gc_recv.at[b, h, c], c, me_h).wait_recv()
+            slot = gathered.at[h, c]
+            remote(slot, slot, gc_send.at[step, o], gc_recv.at[h, c], c, me_h).wait_recv()
 
         loop(1, C, one)
 
-    for b in range(sequences):
-        loop(1, H, lambda o: gz_copy(b, o).start())
-        loop(1, C, lambda o: gc_copy(b, 0, o).start())
-    for b in range(sequences):
-        loop(1, H, lambda step: forward(b, step))
+    loop(1, H, lambda o: gz_copy(o).start())
+    loop(1, C, lambda o: gc_copy(0, o).start())
+    loop(1, H, lambda step: forward(step))
     cache_copy.wait()
 
     def s_copy(b, o):
@@ -244,12 +242,12 @@
     lengths_copy.wait()
     offset = (me_c * H + me_h) * span
     all_heads = queries.shape[1]
-    for b in range(sequences):
-        loop(0, H, lambda step: gc_wait(b, step))
+    loop(0, H, lambda step: gc_wait(step))
+    for b in range(sequences):
         for h in range(H):
             for c in range(C):
                 first = (h * C + c) * own_heads
-                queries[b, first : first + own_heads, :] = gathered[b, h, c].astype(F32)
+                queries[b, first : first + own_heads, :] = gathered[h, c, b].astype(F32)
         usable = (
             offset + lax.broadcasted_iota(jnp.int32, (all_heads, span), 1)
         ) < lengths[b]
@@ -389,9 +387,9 @@
     out[...] = result
 
     loop(1, C, lambda o: p_copy(o).wait_send())
-    for b in range(sequences):
-        loop(1, H, lambda o: gz_copy(b, o).wait_send())
-        loop(0, H, lambda step: loop(1, C, lambda o: gc_copy(b, step, o).wait_send()))
+    loop(1, H, lambda o: gz_copy(o).wait_send())
+    loop(0, H, lambda step: loop(1, C, lambda o: gc_copy(step, o).wait_send()))
+    for b in range(sequences):
         loop(1, C, lambda o: s_copy(b, o).wait_send())
         loop(1, H, lambda o: z_copy(b, o).wait_send())
     loop(1, C, lambda o: v_copy(o).wait_send())
@@ -437,7 +435,7 @@
             vmem((C, sequences, chunk), F32),
             vmem((sequences, chunk), F32),
             vmem((sequences, own_heads, padded), F32),
-            vmem((sequences, H, C, own_heads, padded), BF16),
+            vmem((H, C, sequences, own_heads, padded), BF16),
             vmem((sequences, all_heads, padded), F32),
             vmem((sequences, all_heads, padded), F32),
             vmem((sequences * own_heads, rank), F32),
@@ -454,10 +452,10 @@
             dma((C,)),
             dma((C,)),
             dma((C,)),
-            dma((sequences, H)),
-            dma((sequences, H)),
-            dma((sequences, H, C)),
-            dma((sequences, H, C)),
+            dma((H,)),
+            dma((H,)),
+            dma((H, C)),
+            dma((H, C)),
             dma((sequences, C)),
             dma((sequences, C)),
             dma((sequences, H)),

time: 40.4 us -> 39.7 us (0.983)
  Pallas kernels: 39 us -> 38.3 us
    pallas_call x1, Pallas kernels: 39 us -> 38.3 us  [on_device(): pl.pallas_call(functools.partial(kernel, C, H), out_shape=jax.ShapeDtypeS...]
where the time goes in v4:
time: 39.7 us; the launch traced here: 39.5 us
  Pallas kernels  38.3 us (96%)
  other arithmetic  1.25 us (3%)
    pallas_call x1, Pallas kernels, on_device(): pl.pallas_call(functools.partial(kernel, C, H), out_shape=jax.ShapeDtypeS...  38.3 us
    convert_element_type x1, other arithmetic, on_device(): return result.astype(BF16)  1.25 us

profile of v4, /device:TPU:0, one launch (start us, length us, event | category | flops | bytes accessed | tf_op | source)
XLA Modules:
  0.0 39.5 jit_solution(11147569080431116717)
XLA Ops:
  0.0 38.3 %shard_map.64 = f32[2,224]{1,0:T(2,128)} custom-call(s32[2]{0:T(128)} %lengths_from.1, bf16[2,192]{1,0:T(2,128)(2,1)} %query_low_from.1, bf16[192,18432]{1,0:T(8,128)(2,1)} %query_weight.1, bf16[2,576,1024]{2,1,0:T(8,128)(2,1)} %bitcast.1, bf16[32,512,128]{2,1,0:T(8,128)(2,1)} %value_weight.1, bf16[4096,896]{1,0:T(8,128)(2,1)} %output_weight.1), custom_call_target="tpu_custom_call" | custom-call | tf_op jit(solution)/shard_map/pallas_call | solution.py:414
  38.3 1.2 %convert_element_type.3 = bf16[2,224]{1,0:T(2,128)(2,1)} convert(f32[2,224]{1,0:T(2,128)} %shard_map.64) | non-fusion elementwise | flops 448 | bytes 2688 | tf_op jit(solution)/shard_map/convert_element_type | solution.py:472
